TPU v7x, 32 devices: a whole 2x2x4 slice. The times are simulated.
32 devices in a mesh: pb: 8 (over z, core), tile: 4 (over y, x).
Axes of the slice: x: 2, y: 2, z: 4, core: 2. Of those that a mesh axis runs over, the one named last changes fastest.
Arguments:
- trials: bfloat16 [16, 4, 4096], P('pb', None, 'tile'), may hold values from -6 to 6
- w_screen: bfloat16 [16, 2048, 2048], P('pb', 'tile'), may hold values from -48 to 48
- cond_bands: bfloat16 [16, 2048, 64], P('pb', 'tile'), may hold values from -0.125 to 0.125
- val_bands: bfloat16 [16, 2048, 64], P('pb', 'tile'), may hold values from -0.125 to 0.125
- pair_table: int32 [16, 16], replicated, may hold values from 0 to 15, as said below
Outputs:
- applied: bfloat16 [16, 4, 4096], P('pb', None, 'tile')
Inputs may be any that keep to these rules, and one draw needn't show every extreme that they name: Every row and every column of pair_table holds each k-point exactly once.
All inputs are finite; a program needn't handle non-finite values.
Results may differ from a plain program's by a relative error of at most 0.023.
Values may be sent and summed in bfloat16 or wider, within the bound.
No kernel may reach another device: no remote copies, remote signals or barrier semaphores. Data moves between devices by JAX's collectives and lax.ppermute only.
A program may use at most 128 MiB of HBM per device.

v0:
```python
import functools

import jax
import jax.numpy as jnp
from jax import lax
from jax.experimental import pallas as pl
from jax.experimental.pallas import tpu as pltpu
from jax.sharding import PartitionSpec as P

F32, BF16 = jnp.float32, jnp.bfloat16
ROWS, U0, U1, U3 = 16, 4, 4, 4


def tree_sum(terms):
    while len(terms) > 1:
        half = [terms[i] + terms[i + 1] for i in range(0, len(terms) - 1, 2)]
        terms = half + terms[len(half) * 2 :]
    return terms[0]


def looped(n, unroll, step):
    unroll = unroll if n % unroll == 0 else 1

    def several(i, carry):
        for j in range(unroll):
            step(i * unroll + j)
        return carry

    lax.fori_loop(0, n // unroll, several, 0)


def stage_kernel(kc, rows, pairs, place, uct_ref, x_ref, uvt_ref, *rest):
    *w_refs, yin_ref, y_ref, m_ref, a_ref, e_ref, h_ref, s0_ref, s1_ref = rest
    slots = (s0_ref, s1_ref)
    nk, ns, npts, nblk = m_ref.shape
    qper = w_refs[0].shape[0]
    here = place[0]

    def prepare(k):
        a_ref[k] = lax.dot_general(
            uct_ref[k], x_ref[k], (((0,), (0,)), ((), ())), preferred_element_type=F32
        ).astype(BF16)
        uv = uvt_ref[k].T
        zero = jnp.zeros_like(uv)
        for s in range(ns):
            e_ref[k, s * nblk : (s + 1) * nblk, :] = jnp.concatenate(
                [uv if i == s else zero for i in range(ns)], axis=1
            )

    looped(nk, U0, prepare)

    def mmats(k):
        uvt = uvt_ref[k]
        zero = jnp.zeros_like(uvt)
        for s in range(ns):
            rhs = jnp.concatenate([uvt if i == s else zero for i in range(ns)], axis=0)
            m_ref[k, s] = jnp.dot(a_ref[k], rhs, preferred_element_type=F32).astype(BF16)

    looped(nk, U1, mmats)

    def build(k, slot):
        kreal = ((k // kc) ^ here) * kc + k % kc
        idx = []
        for side in range(len(w_refs)):
            for q in range(qper):
                found = pairs[kreal, (here ^ side) * qper + q]
                idx.append(((found // kc) ^ here) * kc + found % kc)
        for p in range(0, npts, rows):
            wq = [w[q, p : p + rows, :] for w in w_refs for q in range(qper)]
            for s in range(ns):
                slot[p : p + rows, s * nblk : (s + 1) * nblk] = tree_sum(
                    [w * m_ref[i, s, p : p + rows, :] for w, i in zip(wq, idx)]
                )

    def contract(k, slot):
        h_ref[k] = jnp.dot(slot[...], e_ref[k], preferred_element_type=F32).astype(BF16)

    build(0, slots[0])

    def second(i, carry):
        for j in range(4):
            k = 4 * i + j
            contract(k, slots[j % 2])
            build(jnp.minimum(k + 1, nk - 1), slots[1 - j % 2])
        return carry

    lax.fori_loop(0, nk // 4, second, 0)

    def project(k):
        y_ref[k] = yin_ref[k] + jnp.dot(uct_ref[k], h_ref[k], preferred_element_type=F32)

    looped(nk, U3, project)


def stage(step, at_chunk, kc, pairs, place, uct, x, uvt, w_own, w_near, w_far, y):
    nk, _, npts = uct.shape
    nv, nblk = uvt.shape[1:]
    ns = x.shape[2] // nv
    qper = w_own.shape[0]

    def full(a):
        return pl.BlockSpec(a.shape, lambda i, pr, at: (0,) * a.ndim)

    own_spec = pl.BlockSpec(
        (qper, npts, nblk),
        lambda i, pr, at: (0, (at[0] // 2) % 2, (at[1] ^ step) * 2 + at[0] % 2),
    )
    near_spec = pl.BlockSpec((qper, npts, nblk), lambda i, pr, at: (0, 0, step))
    far_spec = pl.BlockSpec((qper, npts, nblk), lambda i, pr, at: (0, 0, at_chunk))
    return pl.pallas_call(
        functools.partial(stage_kernel, kc, ROWS),
        grid_spec=pltpu.PrefetchScalarGridSpec(
            num_scalar_prefetch=2,
            grid=(1,),
            in_specs=[full(uct), full(x), full(uvt), own_spec, near_spec, far_spec, far_spec, full(y)],
            out_specs=full(y),
            scratch_shapes=[
                pltpu.VMEM((nk, ns, npts, nblk), BF16),
                pltpu.VMEM((nk, npts, ns * nv), BF16),
                pltpu.VMEM((nk, ns * nblk, ns * nv), BF16),
                pltpu.VMEM((nk, npts, ns * nv), BF16),
                pltpu.VMEM((npts, ns * nblk), BF16),
                pltpu.VMEM((npts, ns * nblk), BF16),
            ],
        ),
        out_shape=jax.ShapeDtypeStruct(y.shape, F32),
        input_output_aliases={9: 0},
        cost_estimate=pl.CostEstimate(
            flops=16 * nk * ns * npts * nblk * nv, bytes_accessed=32 * qper * npts * nblk, transcendentals=0
        ),
        compiler_params=pltpu.CompilerParams(
            vmem_limit_bytes=40 << 20, dimension_semantics=("arbitrary",)
        ),
    )(pairs, place, uct, x, uvt, w_own, w_near, *w_far, y)


def shards(npb, ntile, trials, w_screen, cond_bands, val_bands, pair_table):
    kc, ns, _ = trials.shape
    _, npts, _ = w_screen.shape
    nc, nv = cond_bands.shape[2], val_bands.shape[2]
    width = val_bands.shape[1]
    half = width // 2
    nk = kc * npb
    cblk = nc // ntile
    here, tile = lax.axis_index("pb"), lax.axis_index("tile")
    core, part = here % 2, (here // 2) % 2
    prow = npts // 2

    def swap(a, axis, d):
        n = npb if axis == "pb" else ntile
        return lax.ppermute(a, axis, [(i, i ^ d) for i in range(n)])

    place = jnp.where(jnp.arange(2) == 0, here, tile).astype(jnp.int32)

    uvh = val_bands.transpose(0, 2, 1)
    lower, upper = uvh[:, :, :half], uvh[:, :, half:]
    uv_got = swap(jnp.where(core == 0, upper, lower), "pb", 1)
    uv_own = jnp.where(core == 0, lower, upper)
    xt = trials.reshape(kc, ns, cblk, nv).transpose(0, 2, 1, 3).reshape(kc, cblk, ns * nv)
    xts = [xt] + [swap(xt, "tile", d) for d in range(1, ntile)]

    ucth = cond_bands.transpose(0, 2, 1)
    first, second = ucth[:, :, :prow], ucth[:, :, prow:]
    uct_mine, uct_other = jnp.where(part == 0, first, second), jnp.where(part == 0, second, first)
    packed = [jnp.concatenate([u, uv_own, uv_got], axis=2) for u in (uct_mine, uct_other)]
    packs = jnp.stack([packed[0]] + [swap(packed[(d // 2) % 2], "pb", d) for d in range(2, npb, 2)])
    x_own = jnp.stack(xts)[jnp.arange(ntile) ^ tile].transpose(1, 0, 2, 3).reshape(kc, nc, ns * nv)
    x_even = jnp.stack([x_own] + [swap(x_own, "pb", d) for d in range(2, npb, 2)])
    even = jnp.concatenate([packs[..., :prow], x_even], axis=3)
    odd = swap(even, "pb", 1)
    both = jnp.stack([even, odd], axis=1).reshape(nk, nc, prow + ns * nv)
    uct, x = both[..., :prow], both[..., prow:]
    uvt = jnp.stack([packs[..., prow : prow + half], packs[..., prow + half :]], axis=1)
    uvt = uvt.reshape(nk, nv, half)
    uvts = [uvt] + [swap(uvt, "tile", d) for d in range(1, ntile)]

    def gated(a, after):
        return lax.optimization_barrier((a, after))[0]

    def w_part(side, steps, source):
        rows = lax.dynamic_slice_in_dim(source, (part ^ (side // 2)) * prow, prow, 1)
        return jnp.concatenate(
            [
                lax.dynamic_slice_in_dim(rows, (tile ^ i) * width + (core ^ (side % 2)) * half, half, 2)
                for i in steps
            ],
            axis=2,
        )

    source = gated(w_screen, packed)
    far_parts = [[w_part(side, [0], source) for side in (2, 3)]]
    near_part = w_part(1, range(ntile), gated(source, far_parts[0]))
    source = gated(source, near_part)
    far_parts += [[w_part(side, [d], source) for side in (2, 3)] for d in range(1, ntile)]
    far = [[swap(cut, "pb", side) for side, cut in zip((2, 3), far_parts[0])]]
    near = swap(near_part, "pb", 1)
    y = jnp.zeros((nk, nc, ns * nv), F32)
    for d in range(ntile):
        if d + 1 < ntile:
            after = packs if d == 0 else y
            far.append([swap(gated(cut, after), "pb", side) for side, cut in zip((2, 3), far_parts[d + 1])])
        y = stage(d, 0, kc, pair_table, place, uct, x, uvts[d], w_screen, near, far[d], y)

    y = y.reshape(npb // 2, 2, kc, nc, ns * nv)
    y = y[:, 0] + swap(y[:, 1].astype(BF16), "pb", 1).astype(F32)
    y = y.reshape(npb // 2, kc, ntile, cblk, ns * nv)

    def block(d):
        return lax.dynamic_index_in_dim(y, tile ^ d, 2, keepdims=False)

    y = sum(
        [swap(block(d).astype(BF16), "tile", d).astype(F32) for d in range(1, ntile)], start=block(0)
    )
    y = sum(
        [swap(y[d].astype(BF16), "pb", 2 * d).astype(F32) for d in range(1, npb // 2)], start=y[0]
    )
    out = y.reshape(kc, cblk, ns, nv).transpose(0, 2, 1, 3)
    return out.reshape(kc, ns, cblk * nv).astype(BF16)


def solution(mesh):
    in_specs = (
        P("pb", None, "tile"),
        P("pb", "tile", None),
        P("pb", "tile", None),
        P("pb", "tile", None),
        P(),
    )
    out_specs = P("pb", None, "tile")

    def body(*args):
        return shards(mesh.shape["pb"], mesh.shape["tile"], *args)

    return jax.shard_map(body, mesh=mesh, in_specs=in_specs, out_specs=out_specs, check_vma=False)
```

profile of v0, /device:TPU:0, one launch (start us, length us, event | category | flops | bytes accessed | tf_op | source)
XLA Modules:
  0.0 128.0 jit_solution(1733008840566772712)
XLA Ops:
  0.9 3.0 %collective-permute-start.4 = (bf16[2,16,256]{2,1,0:T(8,128)(2,1)S(1)}, bf16[2,16,256]{2,1,0:T(8,128)(2,1)S(1)}, u32[]{:S(2)}, u32[]{:S(2)}) collective-permute-start(bf16[2,16,256]{2,1,0:T(8,128)(2,1)S(1)} %reshape.49), channel_id=1, source_target_pairs={{0,1},{1,0},{2,3},{3,2},{4,5},{5,4},{6,7},{7,6},{8,9},{9,8},{10,11... | collective-permute-start | bytes 49160 | tf_op jit(solution)/shard_map/ppermute | solution.py:151
  4.0 1.5 %collective-permute-start.5 = (bf16[2,16,256]{2,1,0:T(8,128)(2,1)S(1)}, bf16[2,16,256]{2,1,0:T(8,128)(2,1)S(1)}, u32[]{:S(2)}, u32[]{:S(2)}) collective-permute-start(bf16[2,16,256]{2,1,0:T(8,128)(2,1)S(1)} %reshape.49), channel_id=1, source_target_pairs={{0,2},{1,3},{2,0},{3,1},{4,6},{5,7},{6,4},{7,5},{8,10},{9,11},{10,... | collective-permute-start | bytes 49160 | tf_op jit(solution)/shard_map/ppermute | solution.py:151
  7.7 2.4 %collective-permute-done.6 = bf16[2,16,256]{2,1,0:T(8,128)(2,1)S(1)} collective-permute-done((bf16[2,16,256]{2,1,0:T(8,128)(2,1)S(1)}, bf16[2,16,256]{2,1,0:T(8,128)(2,1)S(1)}, u32[]{:S(2)}, u32[]{:S(2)}) %collective-permute-start.6) | collective-permute-done | bytes 16416 | tf_op jit(solution)/shard_map/ppermute | solution.py:151
  10.7 1.6 %collective-permute-start.7 = (bf16[2,64,256]{2,1,0:T(8,128)(2,1)S(1)}, bf16[2,64,256]{2,1,0:T(8,128)(2,1)S(1)}, u32[]{:S(2)}, u32[]{:S(2)}) collective-permute-start(bf16[2,64,256]{2,1,0:T(8,128)(2,1)S(1)} %bitcast.87), channel_id=1, source_target_pairs={{0,8},{4,12},{8,0},{12,4},{16,24},{20,28},{24,16},{28,20},{1,9},{5... | collective-permute-start | bytes 196616 | tf_op jit(solution)/shard_map/ppermute | solution.py:151
  12.3 2.6 %collective-permute-start.8 = (bf16[2,64,256]{2,1,0:T(8,128)(2,1)S(1)}, bf16[2,64,256]{2,1,0:T(8,128)(2,1)S(1)}, u32[]{:S(2)}, u32[]{:S(2)}) collective-permute-start(bf16[2,64,256]{2,1,0:T(8,128)(2,1)S(1)} %bitcast.88), channel_id=1, source_target_pairs={{0,16},{4,20},{8,24},{12,28},{16,0},{20,4},{24,8},{28,12},{1,17},{... | collective-permute-start | bytes 196616 | tf_op jit(solution)/shard_map/ppermute | solution.py:151
  15.5 1.3 %collective-permute-start.3 = (bf16[2,64,768]{2,1,0:T(8,128)(2,1)S(1)}, bf16[2,64,768]{2,1,0:T(8,128)(2,1)S(1)}, u32[]{:S(2)}, u32[]{:S(2)}) collective-permute-start(bf16[2,64,768]{2,1,0:T(8,128)(2,1)S(1)} %get-tuple-element.47), channel_id=1, source_target_pairs={{0,24},{4,28},{8,16},{12,20},{16,8},{20,12},{24,0},{28,4},{1,25},{... | collective-permute-start | bytes 589832 | tf_op jit(solution)/shard_map/ppermute | solution.py:151
  16.9 1.7 %collective-permute-start.2 = (bf16[2,64,768]{2,1,0:T(8,128)(2,1)S(1)}, bf16[2,64,768]{2,1,0:T(8,128)(2,1)S(1)}, u32[]{:S(2)}, u32[]{:S(2)}) collective-permute-start(bf16[2,64,768]{2,1,0:T(8,128)(2,1)S(1)} %get-tuple-element.46), channel_id=1, source_target_pairs={{0,16},{4,20},{8,24},{12,28},{16,0},{20,4},{24,8},{28,12},{1,17},{... | collective-permute-start | bytes 589832 | tf_op jit(solution)/shard_map/ppermute | solution.py:151
  18.5 2.2 %constant_dynamic-slice_fusion.10 = (bf16[2,256,256]{2,1,0:T(8,128)(2,1)}, bf16[2,256,256]{2,1,0:T(8,128)(2,1)}) fusion(bf16[2,512,2048]{2,1,0:T(8,128)(2,1)} %rest_0_.7, s32[]{:T(128)S(6)} %select_n.137, s32[]{:T(128)S(6)} %select_n.141, s32[]{:T(128)S(6)} %select_n.139), kind=kLoop, calls=%fused_computation.50 | loop fusion | bytes 1048588 | tf_op jit(solution)/shard_map/dynamic_slice | solution.py:184
  20.8 2.3 %constant_dynamic-slice_fusion.9 = (bf16[2,256,256]{2,1,0:T(8,128)(2,1)S(1)}, bf16[2,256,256]{2,1,0:T(8,128)(2,1)S(1)}, bf16[2,256,256]{2,1,0:T(8,128)(2,1)S(1)}, bf16[2,256,256]{2,1,0:T(8,128)(2,1)S(1)}) fusion(bf16[2,512,2048]{2,1,0:T(8,128)(2,1)} %rest_0_.7, s32[]{:T(128)S(6)} %select_n.143, s32[]{:T(128)S(6)} %select_n.141, s32[]{:T(128)S(6)} %select_n.149, ...), kind=kLoop, calls=%fused_computation.49 | loop fusion | bytes 2097172 | tf_op jit(solution)/shard_map/dynamic_slice | solution.py:184
  24.2 12.9 %collective-permute-done.2 = bf16[2,64,768]{2,1,0:T(8,128)(2,1)S(1)} collective-permute-done((bf16[2,64,768]{2,1,0:T(8,128)(2,1)S(1)}, bf16[2,64,768]{2,1,0:T(8,128)(2,1)S(1)}, u32[]{:S(2)}, u32[]{:S(2)}) %collective-permute-start.2) | collective-permute-done | bytes 196640 | tf_op jit(solution)/shard_map/ppermute | solution.py:151
  40.0 3.1 %constant_dynamic-slice_fusion = (bf16[2,256,256]{2,1,0:T(8,128)(2,1)S(1)}, bf16[2,256,256]{2,1,0:T(8,128)(2,1)S(1)}, bf16[2,256,256]{2,1,0:T(8,128)(2,1)S(1)}, ...) fusion(bf16[2,512,2048]{2,1,0:T(8,128)(2,1)} %rest_0_.7, ...), kind=kLoop, calls=%fused_computation.40 | loop fusion | bytes 3145756 | tf_op jit(solution)/shard_map/dynamic_slice | solution.py:184
  44.2 1.2 collective-permute-start.20
  45.3 1.1 pad_maximum_fusion
  46.7 1.4 %collective-permute-done.16.rest_2_ = bf16[2,256,256]{2,1,0:T(8,128)(2,1)S(1)} collective-permute-done((bf16[2,256,256]{2,1,0:T(8,128)(2,1)}, bf16[2,256,256]{2,1,0:T(8,128)(2,1)S(1)}, u32[]{:S(2)}, u32[]{:S(2)}) %collective-permute-start.16) | collective-permute-done | bytes 262176 | tf_op jit(solution)/shard_map/ppermute | solution.py:151
  48.1 1.3 %collective-permute-start.11 = (bf16[16,64,256]{2,1,0:T(8,128)(2,1)S(1)}, bf16[16,64,256]{2,1,0:T(8,128)(2,1)S(1)}, u32[]{:S(2)}, u32[]{:S(2)}) collective-permute-start(bf16[16,64,256]{2,1,0:T(8,128)(2,1)S(1)} %bitcast.82), channel_id=1, source_target_pairs={{0,3},{1,2},{2,1},{3,0},{4,7},{5,6},{6,5},{7,4},{8,11},{9,10},{10,... | collective-permute-start | bytes 1572872 | tf_op jit(solution)/shard_map/ppermute | solution.py:151
  49.4 2.4 %collective-permute-done.17.rest_3_ = bf16[2,256,256]{2,1,0:T(8,128)(2,1)S(1)} collective-permute-done((bf16[2,256,256]{2,1,0:T(8,128)(2,1)}, bf16[2,256,256]{2,1,0:T(8,128)(2,1)S(1)}, u32[]{:S(2)}, u32[]{:S(2)}) %collective-permute-start.17) | collective-permute-done | bytes 262176 | tf_op jit(solution)/shard_map/ppermute | solution.py:151
  51.8 1.5 %collective-permute-start.14 = (bf16[2,256,256]{2,1,0:T(8,128)(2,1)S(1)}, bf16[2,256,256]{2,1,0:T(8,128)(2,1)S(1)}, u32[]{:S(2)}, u32[]{:S(2)}) collective-permute-start(bf16[2,256,256]{2,1,0:T(8,128)(2,1)S(1)} %get-tuple-element.17), channel_id=1, source_target_pairs={{0,8},{4,12},{8,0},{12,4},{16,24},{20,28},{24,16},{28,20},{1,9},{5... | collective-permute-start | bytes 786440 | tf_op jit(solution)/shard_map/ppermute | solution.py:151
  54.3 13.0 %shard_map.55.rest_4_ = f32[16,64,256]{2,1,0:T(8,128)S(1)} custom-call(s32[16,16]{1,0:T(8,128)S(1)} %copy-done.1, s32[2]{0:T(128)S(1)} %compare_select_fusion.1.place, bf16[16,64,256]{2,1,0:T(8,128)(2,1)S(1)} %get-tuple-element.38.uct_ref, bf16[16,64,256]{2,1,0:T(8,128)(2,1)S(1)} %get-tuple-element.37.x_ref, ...), custom_call_target="tpu_custom_call", output_to_operand_aliasing={{}: (9, {})} | custom-call | flops 4294967296 | bytes 4194304 | tf_op jit(solution)/shard_map/pallas_call | solution.py:110
  67.3 1.1 collective-permute-start.21
  68.4 12.8 %shard_map.56.rest_4_ = f32[16,64,256]{2,1,0:T(8,128)S(1)} custom-call(s32[16,16]{1,0:T(8,128)S(1)} %copy-done.1, s32[2]{0:T(128)S(1)} %compare_select_fusion.1.place, bf16[16,64,256]{2,1,0:T(8,128)(2,1)S(1)} %get-tuple-element.38.uct_ref, bf16[16,64,256]{2,1,0:T(8,128)(2,1)S(1)} %get-tuple-element.37.x_ref, ...), custom_call_target="tpu_custom_call", output_to_operand_aliasing={{}: (9, {})} | custom-call | flops 4294967296 | bytes 4194304 | tf_op jit(solution)/shard_map/pallas_call | solution.py:110
  81.2 1.8 %collective-permute-start.19 = (bf16[2,256,256]{2,1,0:T(8,128)(2,1)S(1)}, bf16[2,256,256]{2,1,0:T(8,128)(2,1)S(1)}, u32[]{:S(2)}, u32[]{:S(2)}) collective-permute-start(bf16[2,256,256]{2,1,0:T(8,128)(2,1)S(1)} %get-tuple-element.20), channel_id=1, source_target_pairs={{0,12},{4,8},{8,4},{12,0},{16,28},{20,24},{24,20},{28,16},{1,13},{... | collective-permute-start | bytes 786440 | tf_op jit(solution)/shard_map/ppermute | solution.py:151
  84.0 12.8 %shard_map.57.rest_4_ = f32[16,64,256]{2,1,0:T(8,128)S(1)} custom-call(s32[16,16]{1,0:T(8,128)S(1)} %copy-done.1, s32[2]{0:T(128)S(1)} %compare_select_fusion.1.place, bf16[16,64,256]{2,1,0:T(8,128)(2,1)S(1)} %get-tuple-element.38.uct_ref, bf16[16,64,256]{2,1,0:T(8,128)(2,1)S(1)} %get-tuple-element.37.x_ref, ...), custom_call_target="tpu_custom_call", output_to_operand_aliasing={{}: (9, {})} | custom-call | flops 4294967296 | bytes 4194304 | tf_op jit(solution)/shard_map/pallas_call | solution.py:110
  96.9 13.0 %shard_map.58 = f32[16,64,256]{2,1,0:T(8,128)S(1)} custom-call(s32[16,16]{1,0:T(8,128)S(1)} %copy-done.1, s32[2]{0:T(128)S(1)} %compare_select_fusion.1.place, bf16[16,64,256]{2,1,0:T(8,128)(2,1)S(1)} %get-tuple-element.38.uct_ref, bf16[16,64,256]{2,1,0:T(8,128)(2,1)S(1)} %get-tuple-element.37.x_ref, ...), custom_call_target="tpu_custom_call", output_to_operand_aliasing={{}: (9, {})} | custom-call | flops 4294967296 | bytes 4194304 | tf_op jit(solution)/shard_map/pallas_call | solution.py:110
  110.1 1.5 %collective-permute-done.23 = bf16[4,2,64,256]{3,2,1,0:T(8,128)(2,1)S(1)} collective-permute-done((bf16[4,2,64,256]{3,2,1,0:T(8,128)(2,1)S(1)}, bf16[4,2,64,256]{3,2,1,0:T(8,128)(2,1)S(1)}, u32[]{:S(2)}, u32[]{:S(2)}) %collective-permute-start.23) | collective-permute-done | bytes 262176 | tf_op jit(solution)/shard_map/ppermute | solution.py:151
  112.6 1.1 collective-permute-start.25
  113.7 1.6 %collective-permute-start.26 = (bf16[4,2,16,256]{3,2,1,0:T(8,128)(2,1)S(1)}, bf16[4,2,16,256]{3,2,1,0:T(8,128)(2,1)S(1)}, u32[]{:S(2)}, u32[]{:S(2)}) collective-permute-start(bf16[4,2,16,256]{3,2,1,0:T(8,128)(2,1)S(1)} %get-tuple-element.43), channel_id=1, source_target_pairs={{0,3},{1,2},{2,1},{3,0},{4,7},{5,6},{6,5},{7,4},{8,11},{9,10},{10,... | collective-permute-start | bytes 196616 | tf_op jit(solution)/shard_map/ppermute | solution.py:151
  116.0 1.6 %collective-permute-done.25 = bf16[4,2,16,256]{3,2,1,0:T(8,128)(2,1)S(1)} collective-permute-done((bf16[4,2,16,256]{3,2,1,0:T(8,128)(2,1)S(1)}, bf16[4,2,16,256]{3,2,1,0:T(8,128)(2,1)S(1)}, u32[]{:S(2)}, u32[]{:S(2)}) %collective-permute-start.25) | collective-permute-done | bytes 65568 | tf_op jit(solution)/shard_map/ppermute | solution.py:151
  117.6 1.3 collective-permute-done.26
  119.9 1.7 %collective-permute-start.28 = (bf16[2,16,256]{2,1,0:T(8,128)(2,1)S(1)}, bf16[2,16,256]{2,1,0:T(8,128)(2,1)S(1)}, u32[]{:S(2)}, u32[]{:S(2)}) collective-permute-start(bf16[2,16,256]{2,1,0:T(8,128)(2,1)S(1)} %get-tuple-element.54), channel_id=1, source_target_pairs={{0,16},{4,20},{8,24},{12,28},{16,0},{20,4},{24,8},{28,12},{1,17},{... | collective-permute-start | bytes 49160 | tf_op jit(solution)/shard_map/ppermute | solution.py:151
  121.6 1.7 %collective-permute-start.29 = (bf16[2,16,256]{2,1,0:T(8,128)(2,1)S(1)}, bf16[2,16,256]{2,1,0:T(8,128)(2,1)S(1)}, u32[]{:S(2)}, u32[]{:S(2)}) collective-permute-start(bf16[2,16,256]{2,1,0:T(8,128)(2,1)S(1)} %get-tuple-element.53), channel_id=1, source_target_pairs={{0,24},{4,28},{8,16},{12,20},{16,8},{20,12},{24,0},{28,4},{1,25},{... | collective-permute-start | bytes 49160 | tf_op jit(solution)/shard_map/ppermute | solution.py:151
  123.3 1.2 collective-permute-done.28
  124.5 2.6 %collective-permute-done.29 = bf16[2,16,256]{2,1,0:T(8,128)(2,1)S(1)} collective-permute-done((bf16[2,16,256]{2,1,0:T(8,128)(2,1)S(1)}, bf16[2,16,256]{2,1,0:T(8,128)(2,1)S(1)}, u32[]{:S(2)}, u32[]{:S(2)}) %collective-permute-start.29) | collective-permute-done | bytes 16416 | tf_op jit(solution)/shard_map/ppermute | solution.py:151
  (80 shorter events, 15.1 us)
Async XLA Ops:
  0.9 6.7 %collective-permute-start.4 = (bf16[2,16,256]{2,1,0:T(8,128)(2,1)S(1)}, bf16[2,16,256]{2,1,0:T(8,128)(2,1)S(1)}, u32[]{:S(2)}, u32[]{:S(2)}) collective-permute-start(bf16[2,16,256]{2,1,0:T(8,128)(2,1)S(1)} %reshape.49), channel_id=1, source_target_pairs={{0,1},{1,0},{2,3},{3,2},{4,5},{5,4},{6,7},{7,6},{8,9},{9,8},{10,11... | collective-permute-start | bytes 49160 | tf_op jit(solution)/shard_map/ppermute | solution.py:151
  4.0 3.7 %collective-permute-start.5 = (bf16[2,16,256]{2,1,0:T(8,128)(2,1)S(1)}, bf16[2,16,256]{2,1,0:T(8,128)(2,1)S(1)}, u32[]{:S(2)}, u32[]{:S(2)}) collective-permute-start(bf16[2,16,256]{2,1,0:T(8,128)(2,1)S(1)} %reshape.49), channel_id=1, source_target_pairs={{0,2},{1,3},{2,0},{3,1},{4,6},{5,7},{6,4},{7,5},{8,10},{9,11},{10,... | collective-permute-start | bytes 49160 | tf_op jit(solution)/shard_map/ppermute | solution.py:151
  5.5 4.6 %collective-permute-start.6 = (bf16[2,16,256]{2,1,0:T(8,128)(2,1)S(1)}, bf16[2,16,256]{2,1,0:T(8,128)(2,1)S(1)}, u32[]{:S(2)}, u32[]{:S(2)}) collective-permute-start(bf16[2,16,256]{2,1,0:T(8,128)(2,1)S(1)} %reshape.49), channel_id=1, source_target_pairs={{0,3},{1,2},{2,1},{3,0},{4,7},{5,6},{6,5},{7,4},{8,11},{9,10},{10,... | collective-permute-start | bytes 49160 | tf_op jit(solution)/shard_map/ppermute | solution.py:151
  6.4 8.6 %collective-permute-start = (bf16[2,64,256]{2,1,0:T(8,128)(2,1)S(1)}, bf16[2,64,256]{2,1,0:T(8,128)(2,1)S(1)}, u32[]{:S(2)}, u32[]{:S(2)}) collective-permute-start(bf16[2,64,256]{2,1,0:T(8,128)(2,1)S(1)} %get-tuple-element.51), channel_id=1, source_target_pairs={{0,4},{4,0},{8,12},{12,8},{16,20},{20,16},{24,28},{28,24},{1,5},{5... | collective-permute-start | bytes 196616 | tf_op jit(solution)/shard_map/ppermute | solution.py:151
  10.7 26.6 %collective-permute-start.7 = (bf16[2,64,256]{2,1,0:T(8,128)(2,1)S(1)}, bf16[2,64,256]{2,1,0:T(8,128)(2,1)S(1)}, u32[]{:S(2)}, u32[]{:S(2)}) collective-permute-start(bf16[2,64,256]{2,1,0:T(8,128)(2,1)S(1)} %bitcast.87), channel_id=1, source_target_pairs={{0,8},{4,12},{8,0},{12,4},{16,24},{20,28},{24,16},{28,20},{1,9},{5... | collective-permute-start | bytes 196616 | tf_op jit(solution)/shard_map/ppermute | solution.py:151
  12.3 24.9 %collective-permute-start.8 = (bf16[2,64,256]{2,1,0:T(8,128)(2,1)S(1)}, bf16[2,64,256]{2,1,0:T(8,128)(2,1)S(1)}, u32[]{:S(2)}, u32[]{:S(2)}) collective-permute-start(bf16[2,64,256]{2,1,0:T(8,128)(2,1)S(1)} %bitcast.88), channel_id=1, source_target_pairs={{0,16},{4,20},{8,24},{12,28},{16,0},{20,4},{24,8},{28,12},{1,17},{... | collective-permute-start | bytes 196616 | tf_op jit(solution)/shard_map/ppermute | solution.py:151
  15.0 8.2 %collective-permute-start.1 = (bf16[2,64,768]{2,1,0:T(8,128)(2,1)S(1)}, bf16[2,64,768]{2,1,0:T(8,128)(2,1)S(1)}, u32[]{:S(2)}, u32[]{:S(2)}) collective-permute-start(bf16[2,64,768]{2,1,0:T(8,128)(2,1)S(1)} %get-tuple-element.47), channel_id=1, source_target_pairs={{0,8},{4,12},{8,0},{12,4},{16,24},{20,28},{24,16},{28,20},{1,9},{5... | collective-permute-start | bytes 589832 | tf_op jit(solution)/shard_map/ppermute | solution.py:151
  15.5 21.6 %collective-permute-start.3 = (bf16[2,64,768]{2,1,0:T(8,128)(2,1)S(1)}, bf16[2,64,768]{2,1,0:T(8,128)(2,1)S(1)}, u32[]{:S(2)}, u32[]{:S(2)}) collective-permute-start(bf16[2,64,768]{2,1,0:T(8,128)(2,1)S(1)} %get-tuple-element.47), channel_id=1, source_target_pairs={{0,24},{4,28},{8,16},{12,20},{16,8},{20,12},{24,0},{28,4},{1,25},{... | collective-permute-start | bytes 589832 | tf_op jit(solution)/shard_map/ppermute | solution.py:151
  16.9 20.2 %collective-permute-start.2 = (bf16[2,64,768]{2,1,0:T(8,128)(2,1)S(1)}, bf16[2,64,768]{2,1,0:T(8,128)(2,1)S(1)}, u32[]{:S(2)}, u32[]{:S(2)}) collective-permute-start(bf16[2,64,768]{2,1,0:T(8,128)(2,1)S(1)} %get-tuple-element.46), channel_id=1, source_target_pairs={{0,16},{4,20},{8,24},{12,28},{16,0},{20,4},{24,8},{28,12},{1,17},{... | collective-permute-start | bytes 589832 | tf_op jit(solution)/shard_map/ppermute | solution.py:151
  23.2 14.1 %collective-permute-start.9 = (bf16[2,64,256]{2,1,0:T(8,128)(2,1)S(1)}, bf16[2,64,256]{2,1,0:T(8,128)(2,1)S(1)}, u32[]{:S(2)}, u32[]{:S(2)}) collective-permute-start(bf16[2,64,256]{2,1,0:T(8,128)(2,1)S(1)} %bitcast.89), channel_id=1, source_target_pairs={{0,24},{4,28},{8,16},{12,20},{16,8},{20,12},{24,0},{28,4},{1,25},{... | collective-permute-start | bytes 196616 | tf_op jit(solution)/shard_map/ppermute | solution.py:151
  37.1 16.2 %collective-permute-start.12 = (bf16[2,256,1024]{2,1,0:T(8,128)(2,1)S(1)}, bf16[2,256,1024]{2,1,0:T(8,128)(2,1)S(1)}, u32[]{:S(2)}, u32[]{:S(2)}) collective-permute-start(bf16[2,256,1024]{2,1,0:T(8,128)(2,1)S(1)} %pad_maximum_fusion.1), channel_id=1, source_target_pairs={{0,4},{4,0},{8,12},{12,8},{16,20},{20,16},{24,28},{28,24},{1,5},{5... | collective-permute-start | bytes 3145736 | tf_op jit(solution)/shard_map/ppermute | solution.py:151
  38.2 6.0 %collective-permute-start.10 = (bf16[4,2,64,512]{3,2,1,0:T(8,128)(2,1)}, bf16[4,2,64,512]{3,2,1,0:T(8,128)(2,1)}, u32[]{:S(2)}, u32[]{:S(2)}) collective-permute-start(bf16[4,2,64,512]{3,2,1,0:T(8,128)(2,1)} %maximum_maximum_fusion), channel_id=1, source_target_pairs={{0,4},{4,0},{8,12},{12,8},{16,20},{20,16},{24,28},{28,24},{1,5},{5... | collective-permute-start | bytes 1572872 | tf_op jit(solution)/shard_map/ppermute | solution.py:151
  38.7 9.4 %collective-permute-start.16 = (bf16[2,256,256]{2,1,0:T(8,128)(2,1)}, bf16[2,256,256]{2,1,0:T(8,128)(2,1)S(1)}, u32[]{:S(2)}, u32[]{:S(2)}) collective-permute-start(bf16[2,256,256]{2,1,0:T(8,128)(2,1)} %get-tuple-element.36), channel_id=1, source_target_pairs={{0,8},{4,12},{8,0},{12,4},{16,24},{20,28},{24,16},{28,20},{1,9},{5... | collective-permute-start | bytes 786440 | tf_op jit(solution)/shard_map/ppermute | solution.py:151
  39.2 12.6 %collective-permute-start.17 = (bf16[2,256,256]{2,1,0:T(8,128)(2,1)}, bf16[2,256,256]{2,1,0:T(8,128)(2,1)S(1)}, u32[]{:S(2)}, u32[]{:S(2)}) collective-permute-start(bf16[2,256,256]{2,1,0:T(8,128)(2,1)} %get-tuple-element.35), channel_id=1, source_target_pairs={{0,12},{4,8},{8,4},{12,0},{16,28},{20,24},{24,20},{28,16},{1,13},{... | collective-permute-start | bytes 786440 | tf_op jit(solution)/shard_map/ppermute | solution.py:151
  43.3 25.2 %collective-permute-start.13 = (bf16[16,64,256]{2,1,0:T(8,128)(2,1)S(1)}, bf16[16,64,256]{2,1,0:T(8,128)(2,1)S(1)}, u32[]{:S(2)}, u32[]{:S(2)}) collective-permute-start(bf16[16,64,256]{2,1,0:T(8,128)(2,1)S(1)} %bitcast.80), channel_id=1, source_target_pairs={{0,1},{1,0},{2,3},{3,2},{4,5},{5,4},{6,7},{7,6},{8,9},{9,8},{10,11... | collective-permute-start | bytes 1572872 | tf_op jit(solution)/shard_map/ppermute | solution.py:151
  44.2 38.9 %collective-permute-start.20 = (bf16[16,64,256]{2,1,0:T(8,128)(2,1)S(1)}, bf16[16,64,256]{2,1,0:T(8,128)(2,1)S(1)}, u32[]{:S(2)}, u32[]{:S(2)}) collective-permute-start(bf16[16,64,256]{2,1,0:T(8,128)(2,1)S(1)} %bitcast.81), channel_id=1, source_target_pairs={{0,2},{1,3},{2,0},{3,1},{4,6},{5,7},{6,4},{7,5},{8,10},{9,11},{10,... | collective-permute-start | bytes 1572872 | tf_op jit(solution)/shard_map/ppermute | solution.py:151
  46.5 7.8 %copy-start = (bf16[2,512,2048]{2,1,0:T(8,128)(2,1)S(1)}, bf16[2,512,2048]{2,1,0:T(8,128)(2,1)}, u32[]{:S(2)}) copy-start(bf16[2,512,2048]{2,1,0:T(8,128)(2,1)} %rest_0_.7) | copy-start | bytes 12582916
  46.6 7.7 %copy-start.1 = (s32[16,16]{1,0:T(8,128)S(1)}, s32[16,16]{1,0:T(8,128)}, u32[]{:S(2)}) copy-start(s32[16,16]{1,0:T(8,128)} %pairs.7) | copy-start | bytes 3076
  48.1 48.8 %collective-permute-start.11 = (bf16[16,64,256]{2,1,0:T(8,128)(2,1)S(1)}, bf16[16,64,256]{2,1,0:T(8,128)(2,1)S(1)}, u32[]{:S(2)}, u32[]{:S(2)}) collective-permute-start(bf16[16,64,256]{2,1,0:T(8,128)(2,1)S(1)} %bitcast.82), channel_id=1, source_target_pairs={{0,3},{1,2},{2,1},{3,0},{4,7},{5,6},{6,5},{7,4},{8,11},{9,10},{10,... | collective-permute-start | bytes 1572872 | tf_op jit(solution)/shard_map/ppermute | solution.py:151
  51.8 15.6 %collective-permute-start.14 = (bf16[2,256,256]{2,1,0:T(8,128)(2,1)S(1)}, bf16[2,256,256]{2,1,0:T(8,128)(2,1)S(1)}, u32[]{:S(2)}, u32[]{:S(2)}) collective-permute-start(bf16[2,256,256]{2,1,0:T(8,128)(2,1)S(1)} %get-tuple-element.17), channel_id=1, source_target_pairs={{0,8},{4,12},{8,0},{12,4},{16,24},{20,28},{24,16},{28,20},{1,9},{5... | collective-permute-start | bytes 786440 | tf_op jit(solution)/shard_map/ppermute | solution.py:151
  53.3 15.1 %collective-permute-start.15 = (bf16[2,256,256]{2,1,0:T(8,128)(2,1)S(1)}, bf16[2,256,256]{2,1,0:T(8,128)(2,1)S(1)}, u32[]{:S(2)}, u32[]{:S(2)}) collective-permute-start(bf16[2,256,256]{2,1,0:T(8,128)(2,1)S(1)} %get-tuple-element.18), channel_id=1, source_target_pairs={{0,12},{4,8},{8,4},{12,0},{16,28},{20,24},{24,20},{28,16},{1,13},{... | collective-permute-start | bytes 786440 | tf_op jit(solution)/shard_map/ppermute | solution.py:151
  67.3 16.7 %collective-permute-start.21 = (bf16[2,256,256]{2,1,0:T(8,128)(2,1)S(1)}, bf16[2,256,256]{2,1,0:T(8,128)(2,1)S(1)}, u32[]{:S(2)}, u32[]{:S(2)}) collective-permute-start(bf16[2,256,256]{2,1,0:T(8,128)(2,1)S(1)} %get-tuple-element.21), channel_id=1, source_target_pairs={{0,8},{4,12},{8,0},{12,4},{16,24},{20,28},{24,16},{28,20},{1,9},{5... | collective-permute-start | bytes 786440 | tf_op jit(solution)/shard_map/ppermute | solution.py:151
  68.4 15.6 %collective-permute-start.22 = (bf16[2,256,256]{2,1,0:T(8,128)(2,1)S(1)}, bf16[2,256,256]{2,1,0:T(8,128)(2,1)S(1)}, u32[]{:S(2)}, u32[]{:S(2)}) collective-permute-start(bf16[2,256,256]{2,1,0:T(8,128)(2,1)S(1)} %get-tuple-element.22), channel_id=1, source_target_pairs={{0,12},{4,8},{8,4},{12,0},{16,28},{20,24},{24,20},{28,16},{1,13},{... | collective-permute-start | bytes 786440 | tf_op jit(solution)/shard_map/ppermute | solution.py:151
  81.2 15.6 %collective-permute-start.19 = (bf16[2,256,256]{2,1,0:T(8,128)(2,1)S(1)}, bf16[2,256,256]{2,1,0:T(8,128)(2,1)S(1)}, u32[]{:S(2)}, u32[]{:S(2)}) collective-permute-start(bf16[2,256,256]{2,1,0:T(8,128)(2,1)S(1)} %get-tuple-element.20), channel_id=1, source_target_pairs={{0,12},{4,8},{8,4},{12,0},{16,28},{20,24},{24,20},{28,16},{1,13},{... | collective-permute-start | bytes 786440 | tf_op jit(solution)/shard_map/ppermute | solution.py:151
  83.0 13.9 %collective-permute-start.18 = (bf16[2,256,256]{2,1,0:T(8,128)(2,1)S(1)}, bf16[2,256,256]{2,1,0:T(8,128)(2,1)S(1)}, u32[]{:S(2)}, u32[]{:S(2)}) collective-permute-start(bf16[2,256,256]{2,1,0:T(8,128)(2,1)S(1)} %get-tuple-element.19), channel_id=1, source_target_pairs={{0,8},{4,12},{8,0},{12,4},{16,24},{20,28},{24,16},{28,20},{1,9},{5... | collective-permute-start | bytes 786440 | tf_op jit(solution)/shard_map/ppermute | solution.py:151
  110.0 1.6 %collective-permute-start.23 = (bf16[4,2,64,256]{3,2,1,0:T(8,128)(2,1)S(1)}, bf16[4,2,64,256]{3,2,1,0:T(8,128)(2,1)S(1)}, u32[]{:S(2)}, u32[]{:S(2)}) collective-permute-start(bf16[4,2,64,256]{3,2,1,0:T(8,128)(2,1)S(1)} %fusion.1), channel_id=1, source_target_pairs={{0,4},{4,0},{8,12},{12,8},{16,20},{20,16},{24,28},{28,24},{1,5},{5... | collective-permute-start | bytes 786440 | tf_op jit(solution)/shard_map/ppermute | solution.py:151
  111.7 4.3 %collective-permute-start.24 = (bf16[4,2,16,256]{3,2,1,0:T(8,128)(2,1)S(1)}, bf16[4,2,16,256]{3,2,1,0:T(8,128)(2,1)S(1)}, u32[]{:S(2)}, u32[]{:S(2)}) collective-permute-start(bf16[4,2,16,256]{3,2,1,0:T(8,128)(2,1)S(1)} %get-tuple-element.42), channel_id=1, source_target_pairs={{0,1},{1,0},{2,3},{3,2},{4,5},{5,4},{6,7},{7,6},{8,9},{9,8},{10,11... | collective-permute-start | bytes 196616 | tf_op jit(solution)/shard_map/ppermute | solution.py:151
  112.6 5.0 %collective-permute-start.25 = (bf16[4,2,16,256]{3,2,1,0:T(8,128)(2,1)S(1)}, bf16[4,2,16,256]{3,2,1,0:T(8,128)(2,1)S(1)}, u32[]{:S(2)}, u32[]{:S(2)}) collective-permute-start(bf16[4,2,16,256]{3,2,1,0:T(8,128)(2,1)S(1)} %get-tuple-element.44), channel_id=1, source_target_pairs={{0,2},{1,3},{2,0},{3,1},{4,6},{5,7},{6,4},{7,5},{8,10},{9,11},{10,... | collective-permute-start | bytes 196616 | tf_op jit(solution)/shard_map/ppermute | solution.py:151
  113.7 5.2 %collective-permute-start.26 = (bf16[4,2,16,256]{3,2,1,0:T(8,128)(2,1)S(1)}, bf16[4,2,16,256]{3,2,1,0:T(8,128)(2,1)S(1)}, u32[]{:S(2)}, u32[]{:S(2)}) collective-permute-start(bf16[4,2,16,256]{3,2,1,0:T(8,128)(2,1)S(1)} %get-tuple-element.43), channel_id=1, source_target_pairs={{0,3},{1,2},{2,1},{3,0},{4,7},{5,6},{6,5},{7,4},{8,11},{9,10},{10,... | collective-permute-start | bytes 196616 | tf_op jit(solution)/shard_map/ppermute | solution.py:151
  118.9 4.5 %collective-permute-start.27 = (bf16[2,16,256]{2,1,0:T(8,128)(2,1)S(1)}, bf16[2,16,256]{2,1,0:T(8,128)(2,1)S(1)}, u32[]{:S(2)}, u32[]{:S(2)}) collective-permute-start(bf16[2,16,256]{2,1,0:T(8,128)(2,1)S(1)} %get-tuple-element.52), channel_id=1, source_target_pairs={{0,8},{4,12},{8,0},{12,4},{16,24},{20,28},{24,16},{28,20},{1,9},{5... | collective-permute-start | bytes 49160 | tf_op jit(solution)/shard_map/ppermute | solution.py:151
  119.9 4.6 %collective-permute-start.28 = (bf16[2,16,256]{2,1,0:T(8,128)(2,1)S(1)}, bf16[2,16,256]{2,1,0:T(8,128)(2,1)S(1)}, u32[]{:S(2)}, u32[]{:S(2)}) collective-permute-start(bf16[2,16,256]{2,1,0:T(8,128)(2,1)S(1)} %get-tuple-element.54), channel_id=1, source_target_pairs={{0,16},{4,20},{8,24},{12,28},{16,0},{20,4},{24,8},{28,12},{1,17},{... | collective-permute-start | bytes 49160 | tf_op jit(solution)/shard_map/ppermute | solution.py:151
  121.6 5.5 %collective-permute-start.29 = (bf16[2,16,256]{2,1,0:T(8,128)(2,1)S(1)}, bf16[2,16,256]{2,1,0:T(8,128)(2,1)S(1)}, u32[]{:S(2)}, u32[]{:S(2)}) collective-permute-start(bf16[2,16,256]{2,1,0:T(8,128)(2,1)S(1)} %get-tuple-element.53), channel_id=1, source_target_pairs={{0,24},{4,28},{8,16},{12,20},{16,8},{20,12},{24,0},{28,4},{1,25},{... | collective-permute-start | bytes 49160 | tf_op jit(solution)/shard_map/ppermute | solution.py:151
  (4 other events, 13.6 us)
where the time goes:
time: 128 us
  Pallas kernels  51.6 us (40%)
  starting transfers between devices  33 us (26%)
  waiting for transfers between devices  28.1 us (22%)
  local copies, waits for them, and re-layouts  10.5 us (8%)
  other arithmetic  4.23 us (3%)
    pallas_call x4, Pallas kernels, stage(): pl.pallas_call(functools.partial(stage_kernel, kc, ROWS), grid_spec=pltpu...  51.6 us
    ppermute x30, starting transfers between devices, swap(): return lax.ppermute(a, axis, [(i, i ^ d) for i in range(n)])  33 us
    ppermute x30, waiting for transfers between devices, swap(): return lax.ppermute(a, axis, [(i, i ^ d) for i in range(n)])  28.1 us
    dynamic_slice x3, local copies, waits for them, and re-layouts, w_part(): lax.dynamic_slice_in_dim(rows, (tile ^ i) * width + (core ^ side % 2) * h...  7.62 us
  transfers between devices with their start and end apart: 30, of which 11 were waited for; matrix products, arithmetic and copies ran while one was open for 10% of the time, Pallas kernels for 30%

commit v1 on v0

--- a/solution.py
+++ b/solution.py
@@ -101,10 +101,6 @@
     def full(a):
         return pl.BlockSpec(a.shape, lambda i, pr, at: (0,) * a.ndim)
 
-    own_spec = pl.BlockSpec(
-        (qper, npts, nblk),
-        lambda i, pr, at: (0, (at[0] // 2) % 2, (at[1] ^ step) * 2 + at[0] % 2),
-    )
     near_spec = pl.BlockSpec((qper, npts, nblk), lambda i, pr, at: (0, 0, step))
     far_spec = pl.BlockSpec((qper, npts, nblk), lambda i, pr, at: (0, 0, at_chunk))
     return pl.pallas_call(
@@ -112,7 +108,7 @@
         grid_spec=pltpu.PrefetchScalarGridSpec(
             num_scalar_prefetch=2,
             grid=(1,),
-            in_specs=[full(uct), full(x), full(uvt), own_spec, near_spec, far_spec, far_spec, full(y)],
+            in_specs=[full(uct), full(x), full(uvt), near_spec, near_spec, far_spec, far_spec, full(y)],
             out_specs=full(y),
             scratch_shapes=[
                 pltpu.VMEM((nk, ns, npts, nblk), BF16),
@@ -192,6 +188,7 @@
     near_part = w_part(1, range(ntile), gated(source, far_parts[0]))
     source = gated(source, near_part)
     far_parts += [[w_part(side, [d], source) for side in (2, 3)] for d in range(1, ntile)]
+    w_own = w_part(0, range(ntile), source)
     far = [[swap(cut, "pb", side) for side, cut in zip((2, 3), far_parts[0])]]
     near = swap(near_part, "pb", 1)
     y = jnp.zeros((nk, nc, ns * nv), F32)
@@ -199,7 +196,7 @@
         if d + 1 < ntile:
             after = packs if d == 0 else y
             far.append([swap(gated(cut, after), "pb", side) for side, cut in zip((2, 3), far_parts[d + 1])])
-        y = stage(d, 0, kc, pair_table, place, uct, x, uvts[d], w_screen, near, far[d], y)
+        y = stage(d, 0, kc, pair_table, place, uct, x, uvts[d], w_own, near, far[d], y)
 
     y = y.reshape(npb // 2, 2, kc, nc, ns * nv)
     y = y[:, 0] + swap(y[:, 1].astype(BF16), "pb", 1).astype(F32)

time: 128 us -> 133 us (1.039)
  Pallas kernels: 51.6 us -> 57.5 us
  waiting for transfers between devices: 28.1 us -> 30.5 us
  other arithmetic: 4.23 us -> 2.52 us
  local copies, waits for them, and re-layouts: 10.5 us -> 9.07 us
    pallas_call x4, Pallas kernels: 51.6 us -> 57.5 us  [stage(): pl.pallas_call(functools.partial(stage_kernel, kc, ROWS), grid_spec=pltpu...]
    ppermute x30, waiting for transfers between devices: 28.1 us -> 30.5 us  [swap(): return lax.ppermute(a, axis, [(i, i ^ d) for i in range(n)])]
    dynamic_slice x3, local copies, waits for them, and re-layouts: 7.62 us -> 6.18 us  [w_part(): lax.dynamic_slice_in_dim(rows, (tile ^ i) * width + (core ^ side % 2) * h...]
  transfers between devices with their start and end apart: 30 -> 30, of which waited for: 11 -> 11; matrix products, arithmetic and copies ran while one was open for 10% -> 7% of each run, Pallas kernels for 30% -> 32%
where the time goes in v1:
time: 133 us
  Pallas kernels  57.5 us (43%)
  starting transfers between devices  32.5 us (24%)
  waiting for transfers between devices  30.5 us (23%)
  local copies, waits for them, and re-layouts  9.07 us (7%)
  other arithmetic  2.52 us (2%)
    pallas_call x4, Pallas kernels, stage(): pl.pallas_call(functools.partial(stage_kernel, kc, ROWS), grid_spec=pltpu...  57.5 us
    ppermute x30, starting transfers between devices, swap(): return lax.ppermute(a, axis, [(i, i ^ d) for i in range(n)])  32.5 us
    ppermute x30, waiting for transfers between devices, swap(): return lax.ppermute(a, axis, [(i, i ^ d) for i in range(n)])  30.5 us
    dynamic_slice x3, local copies, waits for them, and re-layouts, w_part(): lax.dynamic_slice_in_dim(rows, (tile ^ i) * width + (core ^ side % 2) * h...  6.18 us
  transfers between devices with their start and end apart: 30, of which 11 were waited for; matrix products, arithmetic and copies ran while one was open for 7% of the time, Pallas kernels for 32%

profile of v1, /device:TPU:0, one launch (start us, length us, event | category | flops | bytes accessed | tf_op | source)
XLA Modules:
  0.0 132.5 jit_solution(17157525371596485674)
XLA Ops:
  0.9 3.0 %collective-permute-start.4 = (bf16[2,16,256]{2,1,0:T(8,128)(2,1)S(1)}, bf16[2,16,256]{2,1,0:T(8,128)(2,1)S(1)}, u32[]{:S(2)}, u32[]{:S(2)}) collective-permute-start(bf16[2,16,256]{2,1,0:T(8,128)(2,1)S(1)} %reshape.49), channel_id=1, source_target_pairs={{0,1},{1,0},{2,3},{3,2},{4,5},{5,4},{6,7},{7,6},{8,9},{9,8},{10,11... | collective-permute-start | bytes 49160 | tf_op jit(solution)/shard_map/ppermute | solution.py:147
  4.0 1.5 %collective-permute-start.5 = (bf16[2,16,256]{2,1,0:T(8,128)(2,1)S(1)}, bf16[2,16,256]{2,1,0:T(8,128)(2,1)S(1)}, u32[]{:S(2)}, u32[]{:S(2)}) collective-permute-start(bf16[2,16,256]{2,1,0:T(8,128)(2,1)S(1)} %reshape.49), channel_id=1, source_target_pairs={{0,2},{1,3},{2,0},{3,1},{4,6},{5,7},{6,4},{7,5},{8,10},{9,11},{10,... | collective-permute-start | bytes 49160 | tf_op jit(solution)/shard_map/ppermute | solution.py:147
  6.5 0.9 broadcast_select_fusion.3
  7.7 2.4 %collective-permute-done.6 = bf16[2,16,256]{2,1,0:T(8,128)(2,1)S(1)} collective-permute-done((bf16[2,16,256]{2,1,0:T(8,128)(2,1)S(1)}, bf16[2,16,256]{2,1,0:T(8,128)(2,1)S(1)}, u32[]{:S(2)}, u32[]{:S(2)}) %collective-permute-start.6) | collective-permute-done | bytes 16416 | tf_op jit(solution)/shard_map/ppermute | solution.py:147
  10.7 1.6 %collective-permute-start.7 = (bf16[2,64,256]{2,1,0:T(8,128)(2,1)S(1)}, bf16[2,64,256]{2,1,0:T(8,128)(2,1)S(1)}, u32[]{:S(2)}, u32[]{:S(2)}) collective-permute-start(bf16[2,64,256]{2,1,0:T(8,128)(2,1)S(1)} %bitcast.87), channel_id=1, source_target_pairs={{0,8},{4,12},{8,0},{12,4},{16,24},{20,28},{24,16},{28,20},{1,9},{5... | collective-permute-start | bytes 196616 | tf_op jit(solution)/shard_map/ppermute | solution.py:147
  12.3 2.6 %collective-permute-start.8 = (bf16[2,64,256]{2,1,0:T(8,128)(2,1)S(1)}, bf16[2,64,256]{2,1,0:T(8,128)(2,1)S(1)}, u32[]{:S(2)}, u32[]{:S(2)}) collective-permute-start(bf16[2,64,256]{2,1,0:T(8,128)(2,1)S(1)} %bitcast.88), channel_id=1, source_target_pairs={{0,16},{4,20},{8,24},{12,28},{16,0},{20,4},{24,8},{28,12},{1,17},{... | collective-permute-start | bytes 196616 | tf_op jit(solution)/shard_map/ppermute | solution.py:147
  15.5 1.3 %collective-permute-start.3 = (bf16[2,64,768]{2,1,0:T(8,128)(2,1)S(1)}, bf16[2,64,768]{2,1,0:T(8,128)(2,1)S(1)}, u32[]{:S(2)}, u32[]{:S(2)}) collective-permute-start(bf16[2,64,768]{2,1,0:T(8,128)(2,1)S(1)} %get-tuple-element.51), channel_id=1, source_target_pairs={{0,24},{4,28},{8,16},{12,20},{16,8},{20,12},{24,0},{28,4},{1,25},{... | collective-permute-start | bytes 589832 | tf_op jit(solution)/shard_map/ppermute | solution.py:147
  16.9 1.7 %collective-permute-start.2 = (bf16[2,64,768]{2,1,0:T(8,128)(2,1)S(1)}, bf16[2,64,768]{2,1,0:T(8,128)(2,1)S(1)}, u32[]{:S(2)}, u32[]{:S(2)}) collective-permute-start(bf16[2,64,768]{2,1,0:T(8,128)(2,1)S(1)} %get-tuple-element.50), channel_id=1, source_target_pairs={{0,16},{4,20},{8,24},{12,28},{16,0},{20,4},{24,8},{28,12},{1,17},{... | collective-permute-start | bytes 589832 | tf_op jit(solution)/shard_map/ppermute | solution.py:147
  18.5 1.4 %constant_dynamic-slice_fusion.14 = (bf16[2,256,256]{2,1,0:T(8,128)(2,1)S(1)}, bf16[2,256,256]{2,1,0:T(8,128)(2,1)S(1)}) fusion(bf16[2,512,2048]{2,1,0:T(8,128)(2,1)} %param.6, s32[]{:T(128)S(6)} %select_n.142, s32[]{:T(128)S(6)} %select_n.146, s32[]{:T(128)S(6)} %select_n.144), kind=kLoop, calls=%fused_computation.54 | loop fusion | bytes 1048588 | tf_op jit(solution)/shard_map/dynamic_slice | solution.py:180
  20.0 2.3 %constant_dynamic-slice_fusion.13 = (bf16[2,256,256]{2,1,0:T(8,128)(2,1)S(1)}, bf16[2,256,256]{2,1,0:T(8,128)(2,1)S(1)}, bf16[2,256,256]{2,1,0:T(8,128)(2,1)S(1)}, bf16[2,256,256]{2,1,0:T(8,128)(2,1)S(1)}) fusion(bf16[2,512,2048]{2,1,0:T(8,128)(2,1)} %param.6, s32[]{:T(128)S(6)} %select_n.148, s32[]{:T(128)S(6)} %select_n.146, s32[]{:T(128)S(6)} %select_n.154, ...), kind=kLoop, calls=%fused_computation.53 | loop fusion | bytes 2097172 | tf_op jit(solution)/shard_map/dynamic_slice | solution.py:180
  23.4 13.7 %collective-permute-done.2 = bf16[2,64,768]{2,1,0:T(8,128)(2,1)S(1)} collective-permute-done((bf16[2,64,768]{2,1,0:T(8,128)(2,1)S(1)}, bf16[2,64,768]{2,1,0:T(8,128)(2,1)S(1)}, u32[]{:S(2)}, u32[]{:S(2)}) %collective-permute-start.2) | collective-permute-done | bytes 196640 | tf_op jit(solution)/shard_map/ppermute | solution.py:147
  37.4 1.9 %collective-permute-start.17 = (bf16[2,256,256]{2,1,0:T(8,128)(2,1)S(1)}, bf16[2,256,256]{2,1,0:T(8,128)(2,1)S(1)}, u32[]{:S(2)}, u32[]{:S(2)}) collective-permute-start(bf16[2,256,256]{2,1,0:T(8,128)(2,1)S(1)} %get-tuple-element.39), channel_id=1, source_target_pairs={{0,12},{4,8},{8,4},{12,0},{16,28},{20,24},{24,20},{28,16},{1,13},{... | collective-permute-start | bytes 786440 | tf_op jit(solution)/shard_map/ppermute | solution.py:147
  39.7 2.4 %constant_dynamic-slice_fusion = (bf16[2,256,256]{2,1,0:T(8,128)(2,1)S(1)}, bf16[2,256,256]{2,1,0:T(8,128)(2,1)S(1)}, bf16[2,256,256]{2,1,0:T(8,128)(2,1)S(1)}, ...) fusion(bf16[2,512,2048]{2,1,0:T(8,128)(2,1)S(1)} %copy-done.1, ...), kind=kLoop, calls=%fused_computation.40 | loop fusion | bytes 5242916 | tf_op jit(solution)/shard_map/dynamic_slice | solution.py:180
  43.2 1.1 collective-permute-start.20
  44.7 1.6 %collective-permute-done.16.rest_2_ = bf16[2,256,256]{2,1,0:T(8,128)(2,1)S(1)} collective-permute-done((bf16[2,256,256]{2,1,0:T(8,128)(2,1)S(1)}, bf16[2,256,256]{2,1,0:T(8,128)(2,1)S(1)}, u32[]{:S(2)}, u32[]{:S(2)}) %collective-permute-start.16) | collective-permute-done | bytes 262176 | tf_op jit(solution)/shard_map/ppermute | solution.py:147
  46.3 1.3 collective-permute-start.11
  47.6 3.4 %collective-permute-done.17.rest_3_ = bf16[2,256,256]{2,1,0:T(8,128)(2,1)S(1)} collective-permute-done((bf16[2,256,256]{2,1,0:T(8,128)(2,1)S(1)}, bf16[2,256,256]{2,1,0:T(8,128)(2,1)S(1)}, u32[]{:S(2)}, u32[]{:S(2)}) %collective-permute-start.17) | collective-permute-done | bytes 262176 | tf_op jit(solution)/shard_map/ppermute | solution.py:147
  51.6 1.4 %collective-permute-start.15 = (bf16[2,256,256]{2,1,0:T(8,128)(2,1)S(1)}, bf16[2,256,256]{2,1,0:T(8,128)(2,1)S(1)}, u32[]{:S(2)}, u32[]{:S(2)}) collective-permute-start(bf16[2,256,256]{2,1,0:T(8,128)(2,1)S(1)} %get-tuple-element.18), channel_id=1, source_target_pairs={{0,12},{4,8},{8,4},{12,0},{16,28},{20,24},{24,20},{28,16},{1,13},{... | collective-permute-start | bytes 786440 | tf_op jit(solution)/shard_map/ppermute | solution.py:147
  53.0 14.3 %shard_map.55.rest_4_ = f32[16,64,256]{2,1,0:T(8,128)S(1)} custom-call(s32[16,16]{1,0:T(8,128)S(1)} %copy-done, s32[2]{0:T(128)S(1)} %compare_select_fusion.1.place, bf16[16,64,256]{2,1,0:T(8,128)(2,1)S(1)} %get-tuple-element.42.uct_ref, bf16[16,64,256]{2,1,0:T(8,128)(2,1)S(1)} %get-tuple-element.41.x_ref, ...), custom_call_target="tpu_custom_call", output_to_operand_aliasing={{}: (9, {})} | custom-call | flops 4294967296 | bytes 4194304 | tf_op jit(solution)/shard_map/pallas_call | solution.py:106
  67.8 1.3 collective-permute-start.22
  69.0 14.4 %shard_map.56.rest_4_ = f32[16,64,256]{2,1,0:T(8,128)S(1)} custom-call(s32[16,16]{1,0:T(8,128)S(1)} %copy-done, s32[2]{0:T(128)S(1)} %compare_select_fusion.1.place, bf16[16,64,256]{2,1,0:T(8,128)(2,1)S(1)} %get-tuple-element.42.uct_ref, bf16[16,64,256]{2,1,0:T(8,128)(2,1)S(1)} %get-tuple-element.41.x_ref, ...), custom_call_target="tpu_custom_call", output_to_operand_aliasing={{}: (9, {})} | custom-call | flops 4294967296 | bytes 4194304 | tf_op jit(solution)/shard_map/pallas_call | solution.py:106
  84.0 1.7 %collective-permute-start.18 = (bf16[2,256,256]{2,1,0:T(8,128)(2,1)S(1)}, bf16[2,256,256]{2,1,0:T(8,128)(2,1)S(1)}, u32[]{:S(2)}, u32[]{:S(2)}) collective-permute-start(bf16[2,256,256]{2,1,0:T(8,128)(2,1)S(1)} %get-tuple-element.19), channel_id=1, source_target_pairs={{0,8},{4,12},{8,0},{12,4},{16,24},{20,28},{24,16},{28,20},{1,9},{5... | collective-permute-start | bytes 786440 | tf_op jit(solution)/shard_map/ppermute | solution.py:147
  85.7 14.1 %shard_map.57.rest_4_ = f32[16,64,256]{2,1,0:T(8,128)S(1)} custom-call(s32[16,16]{1,0:T(8,128)S(1)} %copy-done, s32[2]{0:T(128)S(1)} %compare_select_fusion.1.place, bf16[16,64,256]{2,1,0:T(8,128)(2,1)S(1)} %get-tuple-element.42.uct_ref, bf16[16,64,256]{2,1,0:T(8,128)(2,1)S(1)} %get-tuple-element.41.x_ref, ...), custom_call_target="tpu_custom_call", output_to_operand_aliasing={{}: (9, {})} | custom-call | flops 4294967296 | bytes 4194304 | tf_op jit(solution)/shard_map/pallas_call | solution.py:106
  99.9 14.6 %shard_map.58 = f32[16,64,256]{2,1,0:T(8,128)S(1)} custom-call(s32[16,16]{1,0:T(8,128)S(1)} %copy-done, s32[2]{0:T(128)S(1)} %compare_select_fusion.1.place, bf16[16,64,256]{2,1,0:T(8,128)(2,1)S(1)} %get-tuple-element.42.uct_ref, bf16[16,64,256]{2,1,0:T(8,128)(2,1)S(1)} %get-tuple-element.41.x_ref, ...), custom_call_target="tpu_custom_call", output_to_operand_aliasing={{}: (9, {})} | custom-call | flops 4294967296 | bytes 4194304 | tf_op jit(solution)/shard_map/pallas_call | solution.py:106
  114.7 1.5 %collective-permute-done.23 = bf16[4,2,64,256]{3,2,1,0:T(8,128)(2,1)S(1)} collective-permute-done((bf16[4,2,64,256]{3,2,1,0:T(8,128)(2,1)S(1)}, bf16[4,2,64,256]{3,2,1,0:T(8,128)(2,1)S(1)}, u32[]{:S(2)}, u32[]{:S(2)}) %collective-permute-start.23) | collective-permute-done | bytes 262176 | tf_op jit(solution)/shard_map/ppermute | solution.py:147
  117.1 1.0 collective-permute-start.25
  118.2 1.7 %collective-permute-start.26 = (bf16[4,2,16,256]{3,2,1,0:T(8,128)(2,1)S(1)}, bf16[4,2,16,256]{3,2,1,0:T(8,128)(2,1)S(1)}, u32[]{:S(2)}, u32[]{:S(2)}) collective-permute-start(bf16[4,2,16,256]{3,2,1,0:T(8,128)(2,1)S(1)} %get-tuple-element.47), channel_id=1, source_target_pairs={{0,3},{1,2},{2,1},{3,0},{4,7},{5,6},{6,5},{7,4},{8,11},{9,10},{10,... | collective-permute-start | bytes 196616 | tf_op jit(solution)/shard_map/ppermute | solution.py:147
  120.6 1.5 %collective-permute-done.25 = bf16[4,2,16,256]{3,2,1,0:T(8,128)(2,1)S(1)} collective-permute-done((bf16[4,2,16,256]{3,2,1,0:T(8,128)(2,1)S(1)}, bf16[4,2,16,256]{3,2,1,0:T(8,128)(2,1)S(1)}, u32[]{:S(2)}, u32[]{:S(2)}) %collective-permute-start.25) | collective-permute-done | bytes 65568 | tf_op jit(solution)/shard_map/ppermute | solution.py:147
  122.1 1.2 collective-permute-done.26
  123.8 2.4 %collective-permute-start.28 = (bf16[2,16,256]{2,1,0:T(8,128)(2,1)S(1)}, bf16[2,16,256]{2,1,0:T(8,128)(2,1)S(1)}, u32[]{:S(2)}, u32[]{:S(2)}) collective-permute-start(bf16[2,16,256]{2,1,0:T(8,128)(2,1)S(1)} %get-tuple-element.58), channel_id=1, source_target_pairs={{0,16},{4,20},{8,24},{12,28},{16,0},{20,4},{24,8},{28,12},{1,17},{... | collective-permute-start | bytes 49160 | tf_op jit(solution)/shard_map/ppermute | solution.py:147
  126.2 1.7 %collective-permute-start.29 = (bf16[2,16,256]{2,1,0:T(8,128)(2,1)S(1)}, bf16[2,16,256]{2,1,0:T(8,128)(2,1)S(1)}, u32[]{:S(2)}, u32[]{:S(2)}) collective-permute-start(bf16[2,16,256]{2,1,0:T(8,128)(2,1)S(1)} %get-tuple-element.57), channel_id=1, source_target_pairs={{0,24},{4,28},{8,16},{12,20},{16,8},{20,12},{24,0},{28,4},{1,25},{... | collective-permute-start | bytes 49160 | tf_op jit(solution)/shard_map/ppermute | solution.py:147
  128.4 3.3 %collective-permute-done.29 = bf16[2,16,256]{2,1,0:T(8,128)(2,1)S(1)} collective-permute-done((bf16[2,16,256]{2,1,0:T(8,128)(2,1)S(1)}, bf16[2,16,256]{2,1,0:T(8,128)(2,1)S(1)}, u32[]{:S(2)}, u32[]{:S(2)}) %collective-permute-start.29) | collective-permute-done | bytes 16416 | tf_op jit(solution)/shard_map/ppermute | solution.py:147
  (73 shorter events, 11.5 us)
Async XLA Ops:
  0.9 6.7 %collective-permute-start.4 = (bf16[2,16,256]{2,1,0:T(8,128)(2,1)S(1)}, bf16[2,16,256]{2,1,0:T(8,128)(2,1)S(1)}, u32[]{:S(2)}, u32[]{:S(2)}) collective-permute-start(bf16[2,16,256]{2,1,0:T(8,128)(2,1)S(1)} %reshape.49), channel_id=1, source_target_pairs={{0,1},{1,0},{2,3},{3,2},{4,5},{5,4},{6,7},{7,6},{8,9},{9,8},{10,11... | collective-permute-start | bytes 49160 | tf_op jit(solution)/shard_map/ppermute | solution.py:147
  4.0 3.7 %collective-permute-start.5 = (bf16[2,16,256]{2,1,0:T(8,128)(2,1)S(1)}, bf16[2,16,256]{2,1,0:T(8,128)(2,1)S(1)}, u32[]{:S(2)}, u32[]{:S(2)}) collective-permute-start(bf16[2,16,256]{2,1,0:T(8,128)(2,1)S(1)} %reshape.49), channel_id=1, source_target_pairs={{0,2},{1,3},{2,0},{3,1},{4,6},{5,7},{6,4},{7,5},{8,10},{9,11},{10,... | collective-permute-start | bytes 49160 | tf_op jit(solution)/shard_map/ppermute | solution.py:147
  5.5 4.6 %collective-permute-start.6 = (bf16[2,16,256]{2,1,0:T(8,128)(2,1)S(1)}, bf16[2,16,256]{2,1,0:T(8,128)(2,1)S(1)}, u32[]{:S(2)}, u32[]{:S(2)}) collective-permute-start(bf16[2,16,256]{2,1,0:T(8,128)(2,1)S(1)} %reshape.49), channel_id=1, source_target_pairs={{0,3},{1,2},{2,1},{3,0},{4,7},{5,6},{6,5},{7,4},{8,11},{9,10},{10,... | collective-permute-start | bytes 49160 | tf_op jit(solution)/shard_map/ppermute | solution.py:147
  6.4 8.6 %collective-permute-start = (bf16[2,64,256]{2,1,0:T(8,128)(2,1)S(1)}, bf16[2,64,256]{2,1,0:T(8,128)(2,1)S(1)}, u32[]{:S(2)}, u32[]{:S(2)}) collective-permute-start(bf16[2,64,256]{2,1,0:T(8,128)(2,1)S(1)} %get-tuple-element.55), channel_id=1, source_target_pairs={{0,4},{4,0},{8,12},{12,8},{16,20},{20,16},{24,28},{28,24},{1,5},{5... | collective-permute-start | bytes 196616 | tf_op jit(solution)/shard_map/ppermute | solution.py:147
  10.7 26.6 %collective-permute-start.7 = (bf16[2,64,256]{2,1,0:T(8,128)(2,1)S(1)}, bf16[2,64,256]{2,1,0:T(8,128)(2,1)S(1)}, u32[]{:S(2)}, u32[]{:S(2)}) collective-permute-start(bf16[2,64,256]{2,1,0:T(8,128)(2,1)S(1)} %bitcast.87), channel_id=1, source_target_pairs={{0,8},{4,12},{8,0},{12,4},{16,24},{20,28},{24,16},{28,20},{1,9},{5... | collective-permute-start | bytes 196616 | tf_op jit(solution)/shard_map/ppermute | solution.py:147
  12.3 26.9 %collective-permute-start.8 = (bf16[2,64,256]{2,1,0:T(8,128)(2,1)S(1)}, bf16[2,64,256]{2,1,0:T(8,128)(2,1)S(1)}, u32[]{:S(2)}, u32[]{:S(2)}) collective-permute-start(bf16[2,64,256]{2,1,0:T(8,128)(2,1)S(1)} %bitcast.88), channel_id=1, source_target_pairs={{0,16},{4,20},{8,24},{12,28},{16,0},{20,4},{24,8},{28,12},{1,17},{... | collective-permute-start | bytes 196616 | tf_op jit(solution)/shard_map/ppermute | solution.py:147
  15.0 7.8 %collective-permute-start.1 = (bf16[2,64,768]{2,1,0:T(8,128)(2,1)S(1)}, bf16[2,64,768]{2,1,0:T(8,128)(2,1)S(1)}, u32[]{:S(2)}, u32[]{:S(2)}) collective-permute-start(bf16[2,64,768]{2,1,0:T(8,128)(2,1)S(1)} %get-tuple-element.51), channel_id=1, source_target_pairs={{0,8},{4,12},{8,0},{12,4},{16,24},{20,28},{24,16},{28,20},{1,9},{5... | collective-permute-start | bytes 589832 | tf_op jit(solution)/shard_map/ppermute | solution.py:147
  15.5 21.6 %collective-permute-start.3 = (bf16[2,64,768]{2,1,0:T(8,128)(2,1)S(1)}, bf16[2,64,768]{2,1,0:T(8,128)(2,1)S(1)}, u32[]{:S(2)}, u32[]{:S(2)}) collective-permute-start(bf16[2,64,768]{2,1,0:T(8,128)(2,1)S(1)} %get-tuple-element.51), channel_id=1, source_target_pairs={{0,24},{4,28},{8,16},{12,20},{16,8},{20,12},{24,0},{28,4},{1,25},{... | collective-permute-start | bytes 589832 | tf_op jit(solution)/shard_map/ppermute | solution.py:147
  16.9 20.3 %collective-permute-start.2 = (bf16[2,64,768]{2,1,0:T(8,128)(2,1)S(1)}, bf16[2,64,768]{2,1,0:T(8,128)(2,1)S(1)}, u32[]{:S(2)}, u32[]{:S(2)}) collective-permute-start(bf16[2,64,768]{2,1,0:T(8,128)(2,1)S(1)} %get-tuple-element.50), channel_id=1, source_target_pairs={{0,16},{4,20},{8,24},{12,28},{16,0},{20,4},{24,8},{28,12},{1,17},{... | collective-permute-start | bytes 589832 | tf_op jit(solution)/shard_map/ppermute | solution.py:147
  22.8 16.4 %collective-permute-start.9 = (bf16[2,64,256]{2,1,0:T(8,128)(2,1)S(1)}, bf16[2,64,256]{2,1,0:T(8,128)(2,1)S(1)}, u32[]{:S(2)}, u32[]{:S(2)}) collective-permute-start(bf16[2,64,256]{2,1,0:T(8,128)(2,1)S(1)} %bitcast.89), channel_id=1, source_target_pairs={{0,24},{4,28},{8,16},{12,20},{16,8},{20,12},{24,0},{28,4},{1,25},{... | collective-permute-start | bytes 196616 | tf_op jit(solution)/shard_map/ppermute | solution.py:147
  37.1 14.4 %collective-permute-start.12 = (bf16[2,256,1024]{2,1,0:T(8,128)(2,1)S(1)}, bf16[2,256,1024]{2,1,0:T(8,128)(2,1)S(1)}, u32[]{:S(2)}, u32[]{:S(2)}) collective-permute-start(bf16[2,256,1024]{2,1,0:T(8,128)(2,1)S(1)} %pad_maximum_fusion.1), channel_id=1, source_target_pairs={{0,4},{4,0},{8,12},{12,8},{16,20},{20,16},{24,28},{28,24},{1,5},{5... | collective-permute-start | bytes 3145736 | tf_op jit(solution)/shard_map/ppermute | solution.py:147
  37.1 9.2 %collective-permute-start.16 = (bf16[2,256,256]{2,1,0:T(8,128)(2,1)S(1)}, bf16[2,256,256]{2,1,0:T(8,128)(2,1)S(1)}, u32[]{:S(2)}, u32[]{:S(2)}) collective-permute-start(bf16[2,256,256]{2,1,0:T(8,128)(2,1)S(1)} %get-tuple-element.40), channel_id=1, source_target_pairs={{0,8},{4,12},{8,0},{12,4},{16,24},{20,28},{24,16},{28,20},{1,9},{5... | collective-permute-start | bytes 786440 | tf_op jit(solution)/shard_map/ppermute | solution.py:147
  37.1 2.5 %copy-start.1 = (bf16[2,512,2048]{2,1,0:T(8,128)(2,1)S(1)}, bf16[2,512,2048]{2,1,0:T(8,128)(2,1)}, u32[]{:S(2)}) copy-start(bf16[2,512,2048]{2,1,0:T(8,128)(2,1)} %param.6) | copy-start | bytes 12582916
  37.4 13.6 %collective-permute-start.17 = (bf16[2,256,256]{2,1,0:T(8,128)(2,1)S(1)}, bf16[2,256,256]{2,1,0:T(8,128)(2,1)S(1)}, u32[]{:S(2)}, u32[]{:S(2)}) collective-permute-start(bf16[2,256,256]{2,1,0:T(8,128)(2,1)S(1)} %get-tuple-element.39), channel_id=1, source_target_pairs={{0,12},{4,8},{8,4},{12,0},{16,28},{20,24},{24,20},{28,16},{1,13},{... | collective-permute-start | bytes 786440 | tf_op jit(solution)/shard_map/ppermute | solution.py:147
  39.3 3.9 %collective-permute-start.10 = (bf16[4,2,64,512]{3,2,1,0:T(8,128)(2,1)S(1)}, bf16[4,2,64,512]{3,2,1,0:T(8,128)(2,1)S(1)}, u32[]{:S(2)}, u32[]{:S(2)}) collective-permute-start(bf16[4,2,64,512]{3,2,1,0:T(8,128)(2,1)S(1)} %maximum_maximum_fusion), channel_id=1, source_target_pairs={{0,4},{4,0},{8,12},{12,8},{16,20},{20,16},{24,28},{28,24},{1,5},{5... | collective-permute-start | bytes 1572872 | tf_op jit(solution)/shard_map/ppermute | solution.py:147
  42.3 26.7 %collective-permute-start.13 = (bf16[16,64,256]{2,1,0:T(8,128)(2,1)S(1)}, bf16[16,64,256]{2,1,0:T(8,128)(2,1)S(1)}, u32[]{:S(2)}, u32[]{:S(2)}) collective-permute-start(bf16[16,64,256]{2,1,0:T(8,128)(2,1)S(1)} %bitcast.80), channel_id=1, source_target_pairs={{0,1},{1,0},{2,3},{3,2},{4,5},{5,4},{6,7},{7,6},{8,9},{9,8},{10,11... | collective-permute-start | bytes 1572872 | tf_op jit(solution)/shard_map/ppermute | solution.py:147
  43.2 40.8 %collective-permute-start.20 = (bf16[16,64,256]{2,1,0:T(8,128)(2,1)S(1)}, bf16[16,64,256]{2,1,0:T(8,128)(2,1)S(1)}, u32[]{:S(2)}, u32[]{:S(2)}) collective-permute-start(bf16[16,64,256]{2,1,0:T(8,128)(2,1)S(1)} %bitcast.81), channel_id=1, source_target_pairs={{0,2},{1,3},{2,0},{3,1},{4,6},{5,7},{6,4},{7,5},{8,10},{9,11},{10,... | collective-permute-start | bytes 1572872 | tf_op jit(solution)/shard_map/ppermute | solution.py:147
  44.5 8.5 %copy-start = (s32[16,16]{1,0:T(8,128)S(1)}, s32[16,16]{1,0:T(8,128)}, u32[]{:S(2)}) copy-start(s32[16,16]{1,0:T(8,128)} %pairs.7) | copy-start | bytes 3076
  46.3 53.6 %collective-permute-start.11 = (bf16[16,64,256]{2,1,0:T(8,128)(2,1)S(1)}, bf16[16,64,256]{2,1,0:T(8,128)(2,1)S(1)}, u32[]{:S(2)}, u32[]{:S(2)}) collective-permute-start(bf16[16,64,256]{2,1,0:T(8,128)(2,1)S(1)} %bitcast.82), channel_id=1, source_target_pairs={{0,3},{1,2},{2,1},{3,0},{4,7},{5,6},{6,5},{7,4},{8,11},{9,10},{10,... | collective-permute-start | bytes 1572872 | tf_op jit(solution)/shard_map/ppermute | solution.py:147
  51.0 16.4 %collective-permute-start.14 = (bf16[2,256,256]{2,1,0:T(8,128)(2,1)S(1)}, bf16[2,256,256]{2,1,0:T(8,128)(2,1)S(1)}, u32[]{:S(2)}, u32[]{:S(2)}) collective-permute-start(bf16[2,256,256]{2,1,0:T(8,128)(2,1)S(1)} %get-tuple-element.17), channel_id=1, source_target_pairs={{0,8},{4,12},{8,0},{12,4},{16,24},{20,28},{24,16},{28,20},{1,9},{5... | collective-permute-start | bytes 786440 | tf_op jit(solution)/shard_map/ppermute | solution.py:147
  51.6 16.2 %collective-permute-start.15 = (bf16[2,256,256]{2,1,0:T(8,128)(2,1)S(1)}, bf16[2,256,256]{2,1,0:T(8,128)(2,1)S(1)}, u32[]{:S(2)}, u32[]{:S(2)}) collective-permute-start(bf16[2,256,256]{2,1,0:T(8,128)(2,1)S(1)} %get-tuple-element.18), channel_id=1, source_target_pairs={{0,12},{4,8},{8,4},{12,0},{16,28},{20,24},{24,20},{28,16},{1,13},{... | collective-permute-start | bytes 786440 | tf_op jit(solution)/shard_map/ppermute | solution.py:147
  67.4 18.3 %collective-permute-start.21 = (bf16[2,256,256]{2,1,0:T(8,128)(2,1)S(1)}, bf16[2,256,256]{2,1,0:T(8,128)(2,1)S(1)}, u32[]{:S(2)}, u32[]{:S(2)}) collective-permute-start(bf16[2,256,256]{2,1,0:T(8,128)(2,1)S(1)} %get-tuple-element.21), channel_id=1, source_target_pairs={{0,8},{4,12},{8,0},{12,4},{16,24},{20,28},{24,16},{28,20},{1,9},{5... | collective-permute-start | bytes 786440 | tf_op jit(solution)/shard_map/ppermute | solution.py:147
  67.8 18.0 %collective-permute-start.22 = (bf16[2,256,256]{2,1,0:T(8,128)(2,1)S(1)}, bf16[2,256,256]{2,1,0:T(8,128)(2,1)S(1)}, u32[]{:S(2)}, u32[]{:S(2)}) collective-permute-start(bf16[2,256,256]{2,1,0:T(8,128)(2,1)S(1)} %get-tuple-element.22), channel_id=1, source_target_pairs={{0,12},{4,8},{8,4},{12,0},{16,28},{20,24},{24,20},{28,16},{1,13},{... | collective-permute-start | bytes 786440 | tf_op jit(solution)/shard_map/ppermute | solution.py:147
  83.4 16.5 %collective-permute-start.19 = (bf16[2,256,256]{2,1,0:T(8,128)(2,1)S(1)}, bf16[2,256,256]{2,1,0:T(8,128)(2,1)S(1)}, u32[]{:S(2)}, u32[]{:S(2)}) collective-permute-start(bf16[2,256,256]{2,1,0:T(8,128)(2,1)S(1)} %get-tuple-element.20), channel_id=1, source_target_pairs={{0,12},{4,8},{8,4},{12,0},{16,28},{20,24},{24,20},{28,16},{1,13},{... | collective-permute-start | bytes 786440 | tf_op jit(solution)/shard_map/ppermute | solution.py:147
  84.0 15.9 %collective-permute-start.18 = (bf16[2,256,256]{2,1,0:T(8,128)(2,1)S(1)}, bf16[2,256,256]{2,1,0:T(8,128)(2,1)S(1)}, u32[]{:S(2)}, u32[]{:S(2)}) collective-permute-start(bf16[2,256,256]{2,1,0:T(8,128)(2,1)S(1)} %get-tuple-element.19), channel_id=1, source_target_pairs={{0,8},{4,12},{8,0},{12,4},{16,24},{20,28},{24,16},{28,20},{1,9},{5... | collective-permute-start | bytes 786440 | tf_op jit(solution)/shard_map/ppermute | solution.py:147
  114.6 1.6 %collective-permute-start.23 = (bf16[4,2,64,256]{3,2,1,0:T(8,128)(2,1)S(1)}, bf16[4,2,64,256]{3,2,1,0:T(8,128)(2,1)S(1)}, u32[]{:S(2)}, u32[]{:S(2)}) collective-permute-start(bf16[4,2,64,256]{3,2,1,0:T(8,128)(2,1)S(1)} %fusion.1), channel_id=1, source_target_pairs={{0,4},{4,0},{8,12},{12,8},{16,20},{20,16},{24,28},{28,24},{1,5},{5... | collective-permute-start | bytes 786440 | tf_op jit(solution)/shard_map/ppermute | solution.py:147
  116.3 4.3 %collective-permute-start.24 = (bf16[4,2,16,256]{3,2,1,0:T(8,128)(2,1)S(1)}, bf16[4,2,16,256]{3,2,1,0:T(8,128)(2,1)S(1)}, u32[]{:S(2)}, u32[]{:S(2)}) collective-permute-start(bf16[4,2,16,256]{3,2,1,0:T(8,128)(2,1)S(1)} %get-tuple-element.46), channel_id=1, source_target_pairs={{0,1},{1,0},{2,3},{3,2},{4,5},{5,4},{6,7},{7,6},{8,9},{9,8},{10,11... | collective-permute-start | bytes 196616 | tf_op jit(solution)/shard_map/ppermute | solution.py:147
  117.1 5.0 %collective-permute-start.25 = (bf16[4,2,16,256]{3,2,1,0:T(8,128)(2,1)S(1)}, bf16[4,2,16,256]{3,2,1,0:T(8,128)(2,1)S(1)}, u32[]{:S(2)}, u32[]{:S(2)}) collective-permute-start(bf16[4,2,16,256]{3,2,1,0:T(8,128)(2,1)S(1)} %get-tuple-element.48), channel_id=1, source_target_pairs={{0,2},{1,3},{2,0},{3,1},{4,6},{5,7},{6,4},{7,5},{8,10},{9,11},{10,... | collective-permute-start | bytes 196616 | tf_op jit(solution)/shard_map/ppermute | solution.py:147
  118.2 5.2 %collective-permute-start.26 = (bf16[4,2,16,256]{3,2,1,0:T(8,128)(2,1)S(1)}, bf16[4,2,16,256]{3,2,1,0:T(8,128)(2,1)S(1)}, u32[]{:S(2)}, u32[]{:S(2)}) collective-permute-start(bf16[4,2,16,256]{3,2,1,0:T(8,128)(2,1)S(1)} %get-tuple-element.47), channel_id=1, source_target_pairs={{0,3},{1,2},{2,1},{3,0},{4,7},{5,6},{6,5},{7,4},{8,11},{9,10},{10,... | collective-permute-start | bytes 196616 | tf_op jit(solution)/shard_map/ppermute | solution.py:147
  123.4 4.5 %collective-permute-start.27 = (bf16[2,16,256]{2,1,0:T(8,128)(2,1)S(1)}, bf16[2,16,256]{2,1,0:T(8,128)(2,1)S(1)}, u32[]{:S(2)}, u32[]{:S(2)}) collective-permute-start(bf16[2,16,256]{2,1,0:T(8,128)(2,1)S(1)} %get-tuple-element.56), channel_id=1, source_target_pairs={{0,8},{4,12},{8,0},{12,4},{16,24},{20,28},{24,16},{28,20},{1,9},{5... | collective-permute-start | bytes 49160 | tf_op jit(solution)/shard_map/ppermute | solution.py:147
  123.8 4.6 %collective-permute-start.28 = (bf16[2,16,256]{2,1,0:T(8,128)(2,1)S(1)}, bf16[2,16,256]{2,1,0:T(8,128)(2,1)S(1)}, u32[]{:S(2)}, u32[]{:S(2)}) collective-permute-start(bf16[2,16,256]{2,1,0:T(8,128)(2,1)S(1)} %get-tuple-element.58), channel_id=1, source_target_pairs={{0,16},{4,20},{8,24},{12,28},{16,0},{20,4},{24,8},{28,12},{1,17},{... | collective-permute-start | bytes 49160 | tf_op jit(solution)/shard_map/ppermute | solution.py:147
  126.2 5.5 %collective-permute-start.29 = (bf16[2,16,256]{2,1,0:T(8,128)(2,1)S(1)}, bf16[2,16,256]{2,1,0:T(8,128)(2,1)S(1)}, u32[]{:S(2)}, u32[]{:S(2)}) collective-permute-start(bf16[2,16,256]{2,1,0:T(8,128)(2,1)S(1)} %get-tuple-element.57), channel_id=1, source_target_pairs={{0,24},{4,28},{8,16},{12,20},{16,8},{20,12},{24,0},{28,4},{1,25},{... | collective-permute-start | bytes 49160 | tf_op jit(solution)/shard_map/ppermute | solution.py:147
